TPU v7x, 256 devices: a whole 4x4x8 slice. The times are simulated.
256 devices in a mesh: orb: 8 (over x, core), dom: 32 (over y, z).
Axes of the slice: x: 4, y: 4, z: 8, core: 2. Of those that a mesh axis runs over, the one named last changes fastest.
Arguments:
- orbitals: float32 [768, 128, 8, 128], P('orb', 'dom'), may hold values from -6 to 6
- potential: float32 [128, 8, 128], P('dom'), may hold values from -1 to 3
- prev_gradient: float32 [768, 128, 8, 128], P('orb', 'dom'), may hold values from -24 to 24
- prev_direction: float32 [768, 128, 8, 128], P('orb', 'dom'), may hold values from -24 to 24
Outputs:
- new_orbitals: float32 [768, 128, 8, 128], P('orb', 'dom')
- new_direction: float32 [768, 128, 8, 128], P('orb', 'dom')
- gradient: float32 [768, 128, 8, 128], P('orb', 'dom')
All inputs are finite; a program needn't handle non-finite values.
Results may differ from a plain program's by a relative error of at most 0.0002.
Values sent between devices are 32-bit elements; how exact they have to be, the bound alone decides.
No kernel may reach another device: no remote copies, remote signals or barrier semaphores. Data moves between devices by JAX's collectives and lax.ppermute only.
A program may use at most 128 MiB of HBM per device.

v0:
```python
import jax
import jax.numpy as jnp
from jax import lax
from jax.sharding import PartitionSpec as P

coeffs = (-205.0 / 72.0, 8.0 / 5.0, -1.0 / 5.0, 8.0 / 315.0, -1.0 / 560.0)
step_length = 0.05


def padded_2(cells, sides, width):
    for axis, dim in sides:
        count = lax.axis_size(axis)
        ends = count - 1
        head = lax.slice_in_dim(cells, 0, width, axis=dim)
        tail = lax.slice_in_dim(cells, cells.shape[dim] - width, cells.shape[dim], axis=dim)
        cells = jnp.concatenate(
            [
                lax.ppermute(tail, axis, [(i, (i + 1) % count) for i in range(ends)]),
                cells,
                lax.ppermute(head, axis, [((i + 1) % count, i) for i in range(ends)]),
            ],
            axis=dim,
        )
    return cells


def laplace(padded, planes, lines, columns):
    center = padded[:, 4 : 4 + planes, 4 : 4 + lines, 4 : 4 + columns]
    total = 3.0 * coeffs[0] * center
    for offset in range(1, 5):
        total = total + coeffs[offset] * (
            padded[:, 4 + offset : 4 + offset + planes, 4 : 4 + lines, 4 : 4 + columns]
            + padded[:, 4 - offset : 4 - offset + planes, 4 : 4 + lines, 4 : 4 + columns]
        )
        total = total + coeffs[offset] * (
            padded[:, 4 : 4 + planes, 4 + offset : 4 + offset + lines, 4 : 4 + columns]
            + padded[:, 4 : 4 + planes, 4 - offset : 4 - offset + lines, 4 : 4 + columns]
        )
        total = total + coeffs[offset] * (
            padded[:, 4 : 4 + planes, 4 : 4 + lines, 4 + offset : 4 + offset + columns]
            + padded[:, 4 : 4 + planes, 4 : 4 + lines, 4 - offset : 4 - offset + columns]
        )
    return total


def highdot(left, right):
    return jnp.dot(left, right, precision=lax.Precision.HIGHEST, preferred_element_type=jnp.float32)


def on_device(orbitals, potential, prev_gradient, prev_direction):
    block = orbitals.shape[0]
    extended = padded_2(orbitals, (("dom", 1),), 4)
    padded = jnp.pad(extended, ((0, 0), (0, 0), (4, 4), (4, 4)))
    lap = laplace(padded, orbitals.shape[1], orbitals.shape[2], orbitals.shape[3])
    image = -0.5 * lap + potential[None] * orbitals
    cmat = orbitals.reshape(block, -1)
    hmat_rows = image.reshape(block, -1)
    cells = cmat.shape[1] * lax.axis_size("dom")
    cell_orbs, cell_images = (
        lax.all_to_all(cmat, "orb", split_axis=1, concat_axis=0, tiled=True),
        lax.all_to_all(hmat_rows, "orb", split_axis=1, concat_axis=0, tiled=True),
    )
    correlation, hamilton = lax.psum(
        (highdot(cell_orbs, cell_orbs.T), highdot(cell_orbs, cell_images.T)), ("orb", "dom")
    )
    correlation = correlation / cells
    hamilton = hamilton / cells
    cell_grad = (
        4.0 * cell_images
        - 2.0 * highdot(correlation.T, cell_images)
        - 2.0 * highdot(hamilton.T, cell_orbs)
    )
    grad = lax.all_to_all(cell_grad, "orb", split_axis=0, concat_axis=1, tiled=True)
    grad = grad.reshape(orbitals.shape)
    both, cross, before = lax.psum(
        (
            jnp.sum(grad * grad),
            jnp.sum(grad * prev_gradient),
            jnp.sum(prev_gradient * prev_gradient),
        ),
        ("orb", "dom"),
    )
    beta = (both - cross) / before
    direction = -grad + beta * prev_direction
    return (orbitals + step_length * direction, direction, grad)


def solution(mesh):
    in_specs = (
        P("orb", "dom", None, None),
        P("dom", None, None),
        P("orb", "dom", None, None),
        P("orb", "dom", None, None),
    )
    out_specs = (
        P("orb", "dom", None, None),
        P("orb", "dom", None, None),
        P("orb", "dom", None, None),
    )
    return jax.shard_map(
        on_device, mesh=mesh, in_specs=in_specs, out_specs=out_specs, check_vma=False
    )
```

profile of v0, /device:TPU:1, one launch (start us, length us, event | category | flops | bytes accessed | tf_op | source)
XLA Modules:
  0.0 553.9 jit_solution(16415115841045701364)
XLA Ops:
  7.2 5.5 collective-permute-start.1
  12.7 1.3 collective-permute-start
  14.0 1.5 all_to_all.44
  15.5 2.1 copy.16
  17.6 5.3 all-to-all-start.1
  22.8 0.0 copy-start
  22.8 22.1 %collective-permute-done.1 = f32[96,4,8,128]{3,2,1,0:T(8,128)} collective-permute-done((f32[96,4,8,128]{3,2,1,0:T(8,128)}, f32[96,4,8,128]{3,2,1,0:T(8,128)}, u32[]{:S(2)}, u32[]{:S(2)}) %collective-permute-start.1) | collective-permute-done | bytes 1572896 | tf_op jit(solution)/shard_map/ppermute | solution.py:18
  44.9 2.7 constant_dynamic-update-slice_fusion.3
  47.6 0.0 copy-done
  47.6 2.1 constant_dynamic-update-slice_fusion.1
  49.8 0.1 collective-permute-done
  49.9 11.4 %select_maximum_fusion = f32[96,12,16,136]{3,2,1,0:T(8,128)} fusion(f32[96,4,8,128]{3,2,1,0:T(8,128)} %collective-permute-done, f32[96,4,8,128]{3,2,1,0:T(8,128)S(1)} %copy-done, f32[96,4,8,128]{3,2,1,0:T(8,128)} %collective-permute-done.1), kind=kLoop, calls=%fused_computation.4 | loop fusion | flops 37601280 | bytes 14745600 | tf_op jit(solution)/shard_map/concatenate | solution.py:16
  61.3 0.0 copy-start.2
  61.3 2.8 constant_dynamic-update-slice_fusion
  64.0 0.0 copy-done.2
  64.0 41.4 %fusion.10 = f32[96,4,8,128]{3,2,1,0:T(8,128)} fusion(f32[96,12,16,136]{3,2,1,0:T(8,128)} %select_maximum_fusion, f32[96,8,8,128]{3,2,1,0:T(8,128)} %get-tuple-element.13, f32[96,8,8,128]{3,2,1,0:T(8,128)} %constant_dynamic-update-slice_fusion, f32[96,4,8,128]{3,2,1,0:T(8,128)S(1)} %copy-done, f32[96,4,8,128]{3,2,1,0:T(8,128)} %collective-permute-done, ...), kind=kLoop, calls=%fused_computation.18 | loop fusion | flops 15728640 | bytes 40910848 | tf_op jit(solution)/shard_map/add | solution.py:55
  105.5 2.6 all_to_all.40
  108.0 3.5 copy.15
  111.5 0.0 all-to-all-done.1
  111.5 6.1 %all-to-all-start = ((f32[96,8,512]{2,0,1:T(8,128)}), f32[96,8,512]{2,0,1:T(8,128)}, u32[]{:S(2)}, u32[]{:S(2)}) async-start(f32[96,8,512]{2,0,1:T(8,128)} %copy.15), calls=%async_computation | async-start | bytes 3145728 | tf_op jit(solution)/shard_map/all_to_all | solution.py:61
  117.6 0.0 all-reduce.5.cloned.1.call-start
  117.6 5.4 fusion.38
  123.0 15.3 %all-to-all-done = f32[96,8,512]{2,0,1:T(8,128)} async-done(((f32[96,8,512]{2,0,1:T(8,128)}), f32[96,8,512]{2,0,1:T(8,128)}, u32[]{:S(2)}, u32[]{:S(2)}) %all-to-all-start) | async-done | bytes 1572896 | tf_op jit(solution)/shard_map/all_to_all | solution.py:61
  138.3 6.8 %convolution_bitcast_fusion = f32[768,768]{1,0:T(8,128)} fusion(f32[768,512]{1,0:T(8,128)} %bitcast.1, f32[768,512]{1,0:T(8,128)S(1)} %bitcast.22), kind=kOutput, calls=%fused_computation.13 | convolution fusion | flops 3623878656 | bytes 5505024 | tf_op jit(solution)/shard_map/dot_general | solution.py:47
  145.1 0.0 all-reduce.5.cloned.1.call-update
  145.1 273.7 %all-reduce.5.cloned.1.call-done = (f32[768,768]{1,0:T(8,128)}, f32[768,768]{1,0:T(8,128)}) async-done(((f32[768,768]{1,0:T(8,128)}, f32[768,768]{1,0:T(8,128)}), (f32[768,768]{1,0:T(8,128)}, f32[768,768]{1,0:T(8,128)})) %all-reduce.5.cloned.1.call-update) | async-done | bytes 4718608 | tf_op jit(solution)/shard_map/psum | solution.py:63
  418.9 0.0 copy-start.1
  418.9 5.7 %fusion.3 = f32[768,512]{1,0:T(8,128)S(1)} fusion(f32[768,512]{1,0:T(8,128)S(1)} %bitcast.23, f32[768,768]{1,0:T(8,128)} %get-tuple-element.8), kind=kOutput, calls=%fused_computation.9 | convolution fusion | flops 3624468480 | bytes 5505024 | tf_op jit(solution)/shard_map/dot_general | solution.py:47
  424.6 0.0 copy-done.1
  424.6 6.3 %multiply_subtract_fusion = f32[768,512]{1,0:T(8,128)S(1)} fusion(f32[768,512]{1,0:T(8,128)S(1)} %fusion.3, f32[768,512]{1,0:T(8,128)} %bitcast.1, f32[768,768]{1,0:T(8,128)S(1)} %copy-done.1), kind=kOutput, calls=%fused_computation.55 | convolution fusion | flops 3626434560 | bytes 7077888 | tf_op jit(solution)/shard_map/dot_general | solution.py:47
  430.9 27.0 %all_to_all.54 = f32[8,96,512]{2,1,0:T(8,128)S(1)} all-to-all(f32[8,96,512]{2,1,0:T(8,128)S(1)} %bitcast.25), channel_id=1, replica_groups=mesh['orb'=8,'dom'=32] {'orb'}, dimensions={0} | all-to-all | bytes 3145728 | tf_op jit(solution)/shard_map/all_to_all | solution.py:73
  457.9 2.1 copy.18
  459.9 2.4 reshape.24
  462.4 2.9 multiply_reduce_fusion
  465.3 1.0 multiply_reduce_fusion.2
  466.3 74.7 %all-reduce.1 = (f32[]{:T(128)}, f32[]{:T(128)}, f32[]{:T(128)}) all-reduce(f32[]{:T(128)} %multiply_reduce_fusion.2, f32[]{:T(128)} %get-tuple-element.4, f32[]{:T(128)} %get-tuple-element.3), channel_id=1, replica_groups=mesh['orb'=8,'dom'=32] {'orb','dom'}, use_global_device_ids=true, to_apply=%region_3.4 | all-reduce | flops 3 | bytes 24 | tf_op jit(solution)/shard_map/psum | solution.py:75
  542.9 4.1 multiply_add_fusion
Async XLA Ops:
  7.2 37.7 %collective-permute-start.1 = (f32[96,4,8,128]{3,2,1,0:T(8,128)}, f32[96,4,8,128]{3,2,1,0:T(8,128)}, u32[]{:S(2)}, u32[]{:S(2)}) collective-permute-start(f32[96,4,8,128]{3,2,1,0:T(8,128)} %param.4), channel_id=1, source_target_pairs={{0,1},{1,2},{2,3},{3,4},{4,5},{5,6},{6,7},{7,8},{8,9},{9,10},{10,1... | collective-permute-start | bytes 4718600 | tf_op jit(solution)/shard_map/ppermute | solution.py:18
  12.7 37.2 %collective-permute-start = (f32[96,4,8,128]{3,2,1,0:T(8,128)}, f32[96,4,8,128]{3,2,1,0:T(8,128)}, u32[]{:S(2)}, u32[]{:S(2)}) collective-permute-start(f32[96,4,8,128]{3,2,1,0:T(8,128)} %param.4), channel_id=1, source_target_pairs={{1,0},{2,1},{3,2},{4,3},{5,4},{6,5},{7,6},{8,7},{9,8},{10,9},{11,1... | collective-permute-start | bytes 4718600 | tf_op jit(solution)/shard_map/ppermute | solution.py:20
  17.6 93.9 %all-to-all-start.1 = ((f32[96,8,512]{2,0,1:T(8,128)}), f32[96,8,512]{2,0,1:T(8,128)S(1)}, u32[]{:S(2)}, u32[]{:S(2)}) async-start(f32[96,8,512]{2,0,1:T(8,128)} %copy.16), calls=%async_computation.1 | async-start | bytes 3145728 | tf_op jit(solution)/shard_map/all_to_all | solution.py:60
  22.8 24.8 %copy-start = (f32[96,4,8,128]{3,2,1,0:T(8,128)S(1)}, f32[96,4,8,128]{3,2,1,0:T(8,128)}, u32[]{:S(2)}) copy-start(f32[96,4,8,128]{3,2,1,0:T(8,128)} %param.4) | copy-start | bytes 4718596
  61.3 2.8 copy-start.2
  111.5 26.8 %all-to-all-start = ((f32[96,8,512]{2,0,1:T(8,128)}), f32[96,8,512]{2,0,1:T(8,128)}, u32[]{:S(2)}, u32[]{:S(2)}) async-start(f32[96,8,512]{2,0,1:T(8,128)} %copy.15), calls=%async_computation | async-start | bytes 3145728 | tf_op jit(solution)/shard_map/all_to_all | solution.py:61
  117.6 301.2 %all-reduce.5.cloned.1.call-start = ((), (), s32[]{:S(2)}) async-start(), calls=%async_computation.3 | async-start | bytes 9437184 | tf_op jit(solution)/shard_map/psum | solution.py:63
  418.9 5.7 %copy-start.1 = (f32[768,768]{1,0:T(8,128)S(1)}, f32[768,768]{1,0:T(8,128)}, u32[]{:S(2)}) copy-start(f32[768,768]{1,0:T(8,128)} %get-tuple-element.9) | copy-start | bytes 7077892
Sparse Core Ops, SparseCore 0:
  145.2 273.5 all-reduce.4
where the time goes:
time: 555 us; the launch traced here: 554 us
  waiting for transfers between devices  311 us (56%)
  blocking collectives  102 us (18%)
  other arithmetic  60.9 us (11%)
  matrix products  24.2 us (4%)
  local copies, waits for them, and re-layouts  21.7 us (4%)
  starting transfers between devices  18.2 us (3%)
  between operations  16 us (3%)
    psum x1, waiting for transfers between devices, on_device(): lax.psum((highdot(cell_orbs, cell_orbs.T), highdot(cell_orbs, cell_images...  274 us
    psum x1, blocking collectives, on_device(): lax.psum((jnp.sum(grad * grad), jnp.sum(grad * prev_gradient), jnp.sum(pr...  74.7 us
    add x1, other arithmetic, on_device(): image = -0.5 * lap + potential[None] * orbitals  41.4 us
    all_to_all x1, blocking collectives, on_device(): lax.all_to_all(cell_grad, 'orb', split_axis=0, concat_axis=1, tiled=True)  27 us
    dot_general x4, matrix products, highdot(): jnp.dot(left, right, precision=lax.Precision.HIGHEST, preferred_element_t...  24.2 us
    ppermute x1, waiting for transfers between devices, padded_2(): lax.ppermute(tail, axis, [(i, (i + 1) % count) for i in range(ends)])  22.1 us
    all_to_all x1, waiting for transfers between devices, on_device(): lax.all_to_all(hmat_rows, 'orb', split_axis=1, concat_axis=0, tiled=True)  15.3 us
    concatenate x1, other arithmetic, padded_2(): jnp.concatenate([lax.ppermute(tail, axis, [(i, (i + 1) % count) for i in...  11.4 us
  transfers between devices with their start and end apart: 5, of which 4 were waited for; matrix products, arithmetic and copies ran while one was open for 13% of the time, Pallas kernels for 0%

commit v1 on v0

--- a/solution.py
+++ b/solution.py
@@ -61,7 +61,7 @@
         lax.all_to_all(hmat_rows, "orb", split_axis=1, concat_axis=0, tiled=True),
     )
     correlation, hamilton = lax.psum(
-        (highdot(cell_orbs, cell_orbs.T), highdot(cell_orbs, cell_images.T)), ("orb", "dom")
+        lax.psum((highdot(cell_orbs, cell_orbs.T), highdot(cell_orbs, cell_images.T)), "dom"), "orb"
     )
     correlation = correlation / cells
     hamilton = hamilton / cells

time: 555 us -> 529 us (0.953)
  waiting for transfers between devices: 311 us -> 285 us
    psum x1, waiting for transfers between devices: 274 us -> 169 us  [on_device(): lax.psum((highdot(cell_orbs, cell_orbs.T), highdot(cell_orbs, cell_images...]
    psum x0 -> x1, waiting for transfers between devices: none -> 78.6 us  [on_device(): lax.psum(lax.psum((highdot(cell_orbs, cell_orbs.T), highdot(cell_orbs, ce...]
  transfers between devices with their start and end apart: 5 -> 6, of which waited for: 4 -> 5; matrix products, arithmetic and copies ran while one was open for 13% -> 13% of each run, Pallas kernels for 0% -> 0%
where the time goes in v1:
time: 529 us; the launch traced here: 528 us
  waiting for transfers between devices  285 us (54%)
  blocking collectives  102 us (19%)
  other arithmetic  60.7 us (11%)
  matrix products  24 us (5%)
  local copies, waits for them, and re-layouts  21.7 us (4%)
  starting transfers between devices  18.4 us (3%)
  between operations  16.1 us (3%)
    psum x1, waiting for transfers between devices, on_device(): lax.psum((highdot(cell_orbs, cell_orbs.T), highdot(cell_orbs, cell_images...  169 us
    psum x1, waiting for transfers between devices, on_device(): lax.psum(lax.psum((highdot(cell_orbs, cell_orbs.T), highdot(cell_orbs, ce...  78.6 us
    psum x1, blocking collectives, on_device(): lax.psum((jnp.sum(grad * grad), jnp.sum(grad * prev_gradient), jnp.sum(pr...  76.4 us
    add x1, other arithmetic, on_device(): image = -0.5 * lap + potential[None] * orbitals  41.3 us
    all_to_all x1, blocking collectives, on_device(): lax.all_to_all(cell_grad, 'orb', split_axis=0, concat_axis=1, tiled=True)  25.9 us
    dot_general x4, matrix products, highdot(): jnp.dot(left, right, precision=lax.Precision.HIGHEST, preferred_element_t...  24 us
    ppermute x1, waiting for transfers between devices, padded_2(): lax.ppermute(tail, axis, [(i, (i + 1) % count) for i in range(ends)])  22.1 us
    all_to_all x1, waiting for transfers between devices, on_device(): lax.all_to_all(hmat_rows, 'orb', split_axis=1, concat_axis=0, tiled=True)  15.3 us
  transfers between devices with their start and end apart: 6, of which 5 were waited for; matrix products, arithmetic and copies ran while one was open for 13% of the time, Pallas kernels for 0%

profile of v1, /device:TPU:1, one launch (start us, length us, event | category | flops | bytes accessed | tf_op | source)
XLA Modules:
  0.0 528.4 jit_solution(14875733334395411901)
XLA Ops:
  7.2 5.5 %collective-permute-start.1 = (f32[96,4,8,128]{3,2,1,0:T(8,128)}, f32[96,4,8,128]{3,2,1,0:T(8,128)}, u32[]{:S(2)}, u32[]{:S(2)}) collective-permute-start(f32[96,4,8,128]{3,2,1,0:T(8,128)} %param.4), channel_id=1, source_target_pairs={{0,1},{1,2},{2,3},{3,4},{4,5},{5,6},{6,7},{7,8},{8,9},{9,10},{10,1... | collective-permute-start | bytes 4718600 | tf_op jit(solution)/shard_map/ppermute | solution.py:18
  12.7 1.3 collective-permute-start
  14.0 1.5 all_to_all.44
  15.5 2.1 copy.16
  17.5 5.3 all-to-all-start.1
  22.8 0.0 copy-start
  22.8 22.1 %collective-permute-done.1 = f32[96,4,8,128]{3,2,1,0:T(8,128)} collective-permute-done((f32[96,4,8,128]{3,2,1,0:T(8,128)}, f32[96,4,8,128]{3,2,1,0:T(8,128)}, u32[]{:S(2)}, u32[]{:S(2)}) %collective-permute-start.1) | collective-permute-done | bytes 1572896 | tf_op jit(solution)/shard_map/ppermute | solution.py:18
  44.9 2.7 constant_dynamic-update-slice_fusion.3
  47.6 0.0 copy-done
  47.6 2.1 constant_dynamic-update-slice_fusion.1
  49.8 0.1 collective-permute-done
  49.9 11.4 %select_maximum_fusion = f32[96,12,16,136]{3,2,1,0:T(8,128)} fusion(f32[96,4,8,128]{3,2,1,0:T(8,128)} %collective-permute-done, f32[96,4,8,128]{3,2,1,0:T(8,128)S(1)} %copy-done, f32[96,4,8,128]{3,2,1,0:T(8,128)} %collective-permute-done.1), kind=kLoop, calls=%fused_computation.4 | loop fusion | flops 37601280 | bytes 14745600 | tf_op jit(solution)/shard_map/concatenate | solution.py:16
  61.3 0.0 copy-start.2
  61.3 2.7 constant_dynamic-update-slice_fusion
  64.0 0.0 copy-done.2
  64.0 41.3 %fusion.10 = f32[96,4,8,128]{3,2,1,0:T(8,128)} fusion(f32[96,12,16,136]{3,2,1,0:T(8,128)} %select_maximum_fusion, f32[96,8,8,128]{3,2,1,0:T(8,128)} %get-tuple-element.15, f32[96,8,8,128]{3,2,1,0:T(8,128)} %constant_dynamic-update-slice_fusion, f32[96,4,8,128]{3,2,1,0:T(8,128)S(1)} %copy-done, f32[96,4,8,128]{3,2,1,0:T(8,128)} %collective-permute-done, ...), kind=kLoop, calls=%fused_computation.18 | loop fusion | flops 15728640 | bytes 40910848 | tf_op jit(solution)/shard_map/add | solution.py:55
  105.3 2.6 all_to_all.40
  107.9 3.5 copy.15
  111.3 0.0 all-to-all-done.1
  111.3 6.1 %all-to-all-start = ((f32[96,8,512]{2,0,1:T(8,128)}), f32[96,8,512]{2,0,1:T(8,128)}, u32[]{:S(2)}, u32[]{:S(2)}) async-start(f32[96,8,512]{2,0,1:T(8,128)} %copy.15), calls=%async_computation | async-start | bytes 3145728 | tf_op jit(solution)/shard_map/all_to_all | solution.py:61
  117.5 0.0 all-reduce.7.cloned.1.call-start
  117.5 5.4 %fusion.38 = f32[768,768]{1,0:T(8,128)} fusion(f32[768,512]{1,0:T(8,128)S(1)} %bitcast.21), kind=kOutput, calls=%fused_computation.64 | convolution fusion | flops 3623878656 | bytes 3932160 | tf_op jit(solution)/shard_map/dot_general | solution.py:47
  122.9 15.3 %all-to-all-done = f32[96,8,512]{2,0,1:T(8,128)} async-done(((f32[96,8,512]{2,0,1:T(8,128)}), f32[96,8,512]{2,0,1:T(8,128)}, u32[]{:S(2)}, u32[]{:S(2)}) %all-to-all-start) | async-done | bytes 1572896 | tf_op jit(solution)/shard_map/all_to_all | solution.py:61
  138.1 6.8 %convolution_bitcast_fusion = f32[768,768]{1,0:T(8,128)} fusion(f32[768,512]{1,0:T(8,128)} %bitcast.1, f32[768,512]{1,0:T(8,128)S(1)} %bitcast.22), kind=kOutput, calls=%fused_computation.13 | convolution fusion | flops 3623878656 | bytes 5505024 | tf_op jit(solution)/shard_map/dot_general | solution.py:47
  144.9 0.0 all-reduce.7.cloned.1.call-update
  145.0 0.3 all-reduce.9.cloned.1.call-start
  145.2 169.2 %all-reduce.7.cloned.1.call-done = (f32[768,768]{1,0:T(8,128)}, f32[768,768]{1,0:T(8,128)}) async-done(((f32[768,768]{1,0:T(8,128)}, f32[768,768]{1,0:T(8,128)}), (f32[768,768]{1,0:T(8,128)}, f32[768,768]{1,0:T(8,128)})) %all-reduce.7.cloned.1.call-update) | async-done | bytes 4718608 | tf_op jit(solution)/shard_map/psum | solution.py:64
  314.4 0.0 all-reduce.9.cloned.1.call-update
  314.4 78.6 %all-reduce.9.cloned.1.call-done = (f32[768,768]{1,0:T(8,128)}, f32[768,768]{1,0:T(8,128)}) async-done(((f32[768,768]{1,0:T(8,128)}, f32[768,768]{1,0:T(8,128)}), (f32[768,768]{1,0:T(8,128)}, f32[768,768]{1,0:T(8,128)})) %all-reduce.9.cloned.1.call-update) | async-done | bytes 4718608 | tf_op jit(solution)/shard_map/psum | solution.py:63
  393.0 0.0 copy-start.1
  393.0 5.7 %fusion.3 = f32[768,512]{1,0:T(8,128)S(1)} fusion(f32[768,512]{1,0:T(8,128)S(1)} %bitcast.23, f32[768,768]{1,0:T(8,128)} %get-tuple-element.10), kind=kOutput, calls=%fused_computation.9 | convolution fusion | flops 3624468480 | bytes 5505024 | tf_op jit(solution)/shard_map/dot_general | solution.py:47
  398.8 0.0 copy-done.1
  398.8 6.0 %multiply_subtract_fusion = f32[768,512]{1,0:T(8,128)S(1)} fusion(f32[768,512]{1,0:T(8,128)S(1)} %fusion.3, f32[768,512]{1,0:T(8,128)} %bitcast.1, f32[768,768]{1,0:T(8,128)S(1)} %copy-done.1), kind=kOutput, calls=%fused_computation.55 | convolution fusion | flops 3626434560 | bytes 7077888 | tf_op jit(solution)/shard_map/dot_general | solution.py:47
  404.8 25.9 %all_to_all.54 = f32[8,96,512]{2,1,0:T(8,128)S(1)} all-to-all(f32[8,96,512]{2,1,0:T(8,128)S(1)} %bitcast.25), channel_id=1, replica_groups=mesh['orb'=8,'dom'=32] {'orb'}, dimensions={0} | all-to-all | bytes 3145728 | tf_op jit(solution)/shard_map/all_to_all | solution.py:73
  430.7 2.1 copy.18
  432.7 2.4 reshape.24
  435.2 2.9 multiply_reduce_fusion
  438.1 1.0 multiply_reduce_fusion.2
  439.1 76.4 %all-reduce.1 = (f32[]{:T(128)}, f32[]{:T(128)}, f32[]{:T(128)}) all-reduce(f32[]{:T(128)} %multiply_reduce_fusion.2, f32[]{:T(128)} %get-tuple-element.4, f32[]{:T(128)} %get-tuple-element.3), channel_id=1, replica_groups=mesh['orb'=8,'dom'=32] {'orb','dom'}, use_global_device_ids=true, to_apply=%region_5.6 | all-reduce | flops 3 | bytes 24 | tf_op jit(solution)/shard_map/psum | solution.py:75
  517.5 4.1 multiply_add_fusion
Async XLA Ops:
  7.2 37.7 %collective-permute-start.1 = (f32[96,4,8,128]{3,2,1,0:T(8,128)}, f32[96,4,8,128]{3,2,1,0:T(8,128)}, u32[]{:S(2)}, u32[]{:S(2)}) collective-permute-start(f32[96,4,8,128]{3,2,1,0:T(8,128)} %param.4), channel_id=1, source_target_pairs={{0,1},{1,2},{2,3},{3,4},{4,5},{5,6},{6,7},{7,8},{8,9},{9,10},{10,1... | collective-permute-start | bytes 4718600 | tf_op jit(solution)/shard_map/ppermute | solution.py:18
  12.7 37.2 %collective-permute-start = (f32[96,4,8,128]{3,2,1,0:T(8,128)}, f32[96,4,8,128]{3,2,1,0:T(8,128)}, u32[]{:S(2)}, u32[]{:S(2)}) collective-permute-start(f32[96,4,8,128]{3,2,1,0:T(8,128)} %param.4), channel_id=1, source_target_pairs={{1,0},{2,1},{3,2},{4,3},{5,4},{6,5},{7,6},{8,7},{9,8},{10,9},{11,1... | collective-permute-start | bytes 4718600 | tf_op jit(solution)/shard_map/ppermute | solution.py:20
  17.5 93.8 %all-to-all-start.1 = ((f32[96,8,512]{2,0,1:T(8,128)}), f32[96,8,512]{2,0,1:T(8,128)S(1)}, u32[]{:S(2)}, u32[]{:S(2)}) async-start(f32[96,8,512]{2,0,1:T(8,128)} %copy.16), calls=%async_computation.1 | async-start | bytes 3145728 | tf_op jit(solution)/shard_map/all_to_all | solution.py:60
  22.8 24.8 %copy-start = (f32[96,4,8,128]{3,2,1,0:T(8,128)S(1)}, f32[96,4,8,128]{3,2,1,0:T(8,128)}, u32[]{:S(2)}) copy-start(f32[96,4,8,128]{3,2,1,0:T(8,128)} %param.4) | copy-start | bytes 4718596
  61.3 2.8 copy-start.2
  111.3 26.8 %all-to-all-start = ((f32[96,8,512]{2,0,1:T(8,128)}), f32[96,8,512]{2,0,1:T(8,128)}, u32[]{:S(2)}, u32[]{:S(2)}) async-start(f32[96,8,512]{2,0,1:T(8,128)} %copy.15), calls=%async_computation | async-start | bytes 3145728 | tf_op jit(solution)/shard_map/all_to_all | solution.py:61
  117.5 196.9 %all-reduce.7.cloned.1.call-start = ((), (), s32[]{:S(2)}) async-start(), calls=%async_computation.3 | async-start | bytes 9437184 | tf_op jit(solution)/shard_map/psum | solution.py:64
  145.0 248.1 %all-reduce.9.cloned.1.call-start = ((), (), s32[]{:S(2)}) async-start(), calls=%async_computation.4 | async-start | bytes 9437184 | tf_op jit(solution)/shard_map/psum | solution.py:63
  393.0 5.7 %copy-start.1 = (f32[768,768]{1,0:T(8,128)S(1)}, f32[768,768]{1,0:T(8,128)}, u32[]{:S(2)}) copy-start(f32[768,768]{1,0:T(8,128)} %get-tuple-element.11) | copy-start | bytes 7077892
Sparse Core Ops, SparseCore 0:
  145.1 169.2 all-reduce.6
  316.8 76.1 all-reduce.8
